TPU v7x, 32 devices: a whole 2x2x4 slice. The times are simulated.
32 devices in a mesh: grp: 4 (over y, x), seq: 8 (over z, core).
Axes of the slice: x: 2, y: 2, z: 4, core: 2. Of those that a mesh axis runs over, the one named last changes fastest.
Arguments:
- tokens: bfloat16 [20480, 1024], P(('grp', 'seq')), may hold values from -6 to 6
- cotangent: bfloat16 [20480, 1024], P(('grp', 'seq')), may hold values from -6 to 6
- query_key_value_weight: bfloat16 [3145728], P(('grp', 'seq')), may hold values from -0.1875 to 0.1875
- attention_out_weight: bfloat16 [1048576], P(('grp', 'seq')), may hold values from -1.5 to 1.5
- feedforward_in_weight: bfloat16 [4194304], P(('grp', 'seq')), may hold values from -0.1875 to 0.1875
- feedforward_out_weight: bfloat16 [4194304], P(('grp', 'seq')), may hold values from -0.09375 to 0.09375
- layer_norm_gains: float32 [2, 1024], replicated, may hold values from 0.25 to 1.75
- biases: float32 [10240], replicated, may hold values from -1.75 to 1.75
- adapter_down_matrices: bfloat16 [917504], P(('grp', 'seq')), may hold values from -0.1875 to 0.1875
- adapter_up_matrices: bfloat16 [1179648], P(('grp', 'seq')), may hold values from -0.75 to 0.75
- adapter_of_continuation: int32 [32, 1], P(('grp', 'seq')), may hold values from 0 to 7
Outputs:
- activations: bfloat16 [20480, 1024], P(('grp', 'seq'))
- input_grad: float32 [20480, 1024], P(('grp', 'seq'))
- down_grad: float32 [917504], P(('grp', 'seq'))
- up_grad: float32 [1179648], P(('grp', 'seq'))
Inputs may be any that keep to these rules, and one draw needn't show every extreme that they name: `adapter_of_continuation`: every one of the 8 adapters is named by some continuation.
All inputs are finite; a program needn't handle non-finite values.
Results may differ from a plain program's by a relative error of at most 0.012.
Values may be sent and summed in bfloat16 or wider, within the bound.
A program may use at most 256 MiB of HBM per device.

v0:
```python
import jax
import jax.numpy as jnp
from jax import lax
from jax.sharding import PartitionSpec as P

MODEL_WIDTH = 1024
HEADS = 16
HEAD_DIM = 64
HIDDEN_UNITS = 4096
ADAPTER_RANK = 16
ADAPTER_COUNT = 8
CONT_LEN = 512


EPSILON = 1e-05
NEGATIVE = -1e30


def product(left_side, right_side):
    return jnp.dot(left_side, right_side, preferred_element_type=jnp.float32)


def product_tn(left_side, right_side):
    return lax.dot_general(
        left_side, right_side, (((0,), (0,)), ((), ())), preferred_element_type=jnp.float32
    )


def product_nt(left_side, right_side):
    return lax.dot_general(
        left_side, right_side, (((1,), (1,)), ((), ())), preferred_element_type=jnp.float32
    )


def layer_norm(values, gain_vec, shift_vec):
    row_mean = jnp.mean(values, axis=-1, keepdims=True)
    centred = values - row_mean
    row_var = jnp.mean(centred * centred, axis=-1, keepdims=True)
    return centred * lax.rsqrt(row_var + EPSILON) * gain_vec + shift_vec


def unpack_sections(pieces, adapter_index):
    qkv_flat, out_flat, fc_flat, proj_flat, down_flat, up_flat = pieces
    every_down_matrix = down_flat.reshape(
        ADAPTER_COUNT, 3 * MODEL_WIDTH + HIDDEN_UNITS, ADAPTER_RANK
    )
    every_up_matrix = up_flat.reshape(ADAPTER_COUNT, ADAPTER_RANK, 5 * MODEL_WIDTH + HIDDEN_UNITS)
    down_rows = lax.dynamic_index_in_dim(every_down_matrix, adapter_index, 0, keepdims=False)
    up_cols = lax.dynamic_index_in_dim(every_up_matrix, adapter_index, 0, keepdims=False)
    weight_matrices = (
        qkv_flat.reshape(MODEL_WIDTH, 3 * MODEL_WIDTH),
        out_flat.reshape(MODEL_WIDTH, MODEL_WIDTH),
        fc_flat.reshape(MODEL_WIDTH, HIDDEN_UNITS),
        proj_flat.reshape(HIDDEN_UNITS, MODEL_WIDTH),
    )
    adapter_sections = (
        down_rows[:MODEL_WIDTH],
        down_rows[MODEL_WIDTH : 2 * MODEL_WIDTH],
        down_rows[2 * MODEL_WIDTH : 3 * MODEL_WIDTH],
        down_rows[3 * MODEL_WIDTH :],
        up_cols[:, : 3 * MODEL_WIDTH],
        up_cols[:, 3 * MODEL_WIDTH : 4 * MODEL_WIDTH],
        up_cols[:, 4 * MODEL_WIDTH : 4 * MODEL_WIDTH + HIDDEN_UNITS],
        up_cols[:, 4 * MODEL_WIDTH + HIDDEN_UNITS :],
    )
    return (weight_matrices, adapter_sections)


def visible(row_count, prompt_rows, prompt_total, key_count, seq_index):
    row_ids = jnp.arange(row_count, dtype=jnp.int32)[:, None]
    col_ids = jnp.arange(key_count, dtype=jnp.int32)[None, :]
    in_prompt = col_ids < prompt_total
    prompt_seen = in_prompt & (col_ids <= seq_index * prompt_rows + row_ids)
    later_seen = in_prompt | (col_ids - prompt_total <= row_ids - prompt_rows)
    return jnp.where(row_ids < prompt_rows, prompt_seen, later_seen)


def split_heads(values):
    return values.reshape(values.shape[0], HEADS, HEAD_DIM).transpose(1, 0, 2)


def merge_heads(values):
    return values.transpose(1, 0, 2).reshape(values.shape[1], HEADS * HEAD_DIM)


def local(
    tokens,
    cotangent,
    query_key_value_weight,
    attention_out_weight,
    feedforward_in_weight,
    feedforward_out_weight,
    layer_norm_gains,
    biases,
    adapter_down_matrices,
    adapter_up_matrices,
    adapter_of_continuation,
):
    row_count = tokens.shape[0]
    prompt_rows = row_count - CONT_LEN
    prompt_total = prompt_rows * lax.axis_size("seq")
    key_count = prompt_total + CONT_LEN
    seq_index = lax.axis_index("seq")
    adapter_index = adapter_of_continuation[0, 0]
    weight_shards = (
        query_key_value_weight,
        attention_out_weight,
        feedforward_in_weight,
        feedforward_out_weight,
        adapter_down_matrices,
        adapter_up_matrices,
    )
    gathered_rows = (
        lax.all_gather(weight_shards[0], ("grp", "seq"), axis=0, tiled=True),
        lax.all_gather(weight_shards[1], ("grp", "seq"), axis=0, tiled=True),
        lax.all_gather(weight_shards[2], ("grp", "seq"), axis=0, tiled=True),
        lax.all_gather(weight_shards[3], ("grp", "seq"), axis=0, tiled=True),
        lax.all_gather(weight_shards[4], ("grp", "seq"), axis=0, tiled=True),
        lax.all_gather(weight_shards[5], ("grp", "seq"), axis=0, tiled=True),
    )
    weight_matrices, adapter_sections = unpack_sections(gathered_rows, adapter_index)
    frozen_query_key_value, frozen_attention_out, frozen_feedforward_in, frozen_feedforward_out = (
        weight_matrices
    )
    (
        down_query_key_value,
        down_attention_out,
        down_feedforward_in,
        down_feedforward_out,
        up_query_key_value,
        up_attention_out,
        up_feedforward_in,
        up_feedforward_out,
    ) = adapter_sections
    shift_one = biases[:MODEL_WIDTH]
    shift_two = biases[MODEL_WIDTH : 2 * MODEL_WIDTH]
    query_key_value_bias = jnp.concatenate(
        [
            biases[2 * MODEL_WIDTH : 3 * MODEL_WIDTH],
            jnp.zeros((MODEL_WIDTH,), jnp.float32),
            biases[3 * MODEL_WIDTH : 4 * MODEL_WIDTH],
        ]
    )
    bias_out = biases[4 * MODEL_WIDTH : 5 * MODEL_WIDTH]
    bias_proj = biases[5 * MODEL_WIDTH : 6 * MODEL_WIDTH]
    bias_fc = biases[6 * MODEL_WIDTH :]
    inputs = tokens.astype(jnp.float32)
    normed_one = layer_norm(inputs, layer_norm_gains[0], shift_one).astype(jnp.bfloat16)
    inner_one = product(normed_one[prompt_rows:], down_query_key_value).astype(jnp.bfloat16)
    mixed_query_key_value = product(normed_one, frozen_query_key_value) + query_key_value_bias
    mixed_query_key_value = mixed_query_key_value.at[prompt_rows:].add(
        product(inner_one, up_query_key_value)
    )
    qkv_rows = mixed_query_key_value.astype(jnp.bfloat16)
    prompt_keys, prompt_values = (
        lax.all_gather(
            qkv_rows[:prompt_rows, MODEL_WIDTH : 2 * MODEL_WIDTH], "seq", axis=0, tiled=True
        ),
        lax.all_gather(qkv_rows[:prompt_rows, 2 * MODEL_WIDTH :], "seq", axis=0, tiled=True),
    )
    all_keys = jnp.concatenate(
        [prompt_keys, qkv_rows[prompt_rows:, MODEL_WIDTH : 2 * MODEL_WIDTH]], 0
    )
    all_values = jnp.concatenate([prompt_values, qkv_rows[prompt_rows:, 2 * MODEL_WIDTH :]], 0)
    allowed = visible(row_count, prompt_rows, prompt_total, key_count, seq_index)
    query_heads = split_heads(qkv_rows[:, :MODEL_WIDTH])
    key_heads = split_heads(all_keys)
    value_heads = split_heads(all_values)

    def forward_head(operands):
        query_head, key_head, value_head = operands
        scores = jnp.where(allowed, product_nt(query_head, key_head) * 0.125, NEGATIVE)
        row_max = jnp.max(scores, axis=1, keepdims=True)
        exp_scores = jnp.exp(scores - row_max)
        exp_total = jnp.sum(exp_scores, axis=1, keepdims=True)
        weights = (exp_scores / exp_total).astype(jnp.bfloat16)
        return (product(weights, value_head), (row_max + jnp.log(exp_total))[:, 0])

    head_contexts, log_total = lax.map(forward_head, (query_heads, key_heads, value_heads))
    attention_context = merge_heads(head_contexts).astype(jnp.bfloat16)
    inner_two = product(attention_context[prompt_rows:], down_attention_out).astype(jnp.bfloat16)
    attention_output = product(attention_context, frozen_attention_out) + bias_out
    attention_output = attention_output.at[prompt_rows:].add(product(inner_two, up_attention_out))
    hidden = inputs + attention_output
    normed_two = layer_norm(hidden, layer_norm_gains[1], shift_two).astype(jnp.bfloat16)
    inner_three = product(normed_two[prompt_rows:], down_feedforward_in).astype(jnp.bfloat16)
    before_activation = product(normed_two, frozen_feedforward_in) + bias_fc
    before_activation = before_activation.at[prompt_rows:].add(
        product(inner_three, up_feedforward_in)
    )
    activated_hidden = jax.nn.gelu(before_activation, approximate=True).astype(jnp.bfloat16)
    inner_four = product(activated_hidden[prompt_rows:], down_feedforward_out).astype(jnp.bfloat16)
    adapter_branch = product(activated_hidden, frozen_feedforward_out) + bias_proj
    adapter_branch = adapter_branch.at[prompt_rows:].add(product(inner_four, up_feedforward_out))
    outputs = (hidden + adapter_branch).astype(jnp.bfloat16)
    weight_matrices, adapter_sections = unpack_sections(
        (
            lax.all_gather(weight_shards[0], ("grp", "seq"), axis=0, tiled=True),
            lax.all_gather(weight_shards[1], ("grp", "seq"), axis=0, tiled=True),
            lax.all_gather(weight_shards[2], ("grp", "seq"), axis=0, tiled=True),
            lax.all_gather(weight_shards[3], ("grp", "seq"), axis=0, tiled=True),
            lax.all_gather(weight_shards[4], ("grp", "seq"), axis=0, tiled=True),
            lax.all_gather(weight_shards[5], ("grp", "seq"), axis=0, tiled=True),
        ),
        adapter_index,
    )
    frozen_query_key_value, frozen_attention_out, frozen_feedforward_in, frozen_feedforward_out = (
        weight_matrices
    )
    (
        down_query_key_value,
        down_attention_out,
        down_feedforward_in,
        down_feedforward_out,
        up_query_key_value,
        up_attention_out,
        up_feedforward_in,
        up_feedforward_out,
    ) = adapter_sections
    grad_inner_four = product_nt(cotangent[prompt_rows:], up_feedforward_out).astype(jnp.bfloat16)
    grad_act = product_nt(cotangent, frozen_feedforward_out)
    grad_act = grad_act.at[prompt_rows:].add(product_nt(grad_inner_four, down_feedforward_out))
    gelu_pull = jax.vjp(lambda field: jax.nn.gelu(field, approximate=True), before_activation)[1]
    grad_pre = gelu_pull(grad_act)[0].astype(jnp.bfloat16)
    grad_inner_three = product_nt(grad_pre[prompt_rows:], up_feedforward_in).astype(jnp.bfloat16)
    grad_normed_two = product_nt(grad_pre, frozen_feedforward_in)
    grad_normed_two = grad_normed_two.at[prompt_rows:].add(
        product_nt(grad_inner_three, down_feedforward_in)
    )
    second_pull = jax.vjp(lambda field: layer_norm(field, layer_norm_gains[1], shift_two), hidden)[
        1
    ]
    grad_hidden = cotangent.astype(jnp.float32) + second_pull(grad_normed_two)[0]
    grad_attn = grad_hidden.astype(jnp.bfloat16)
    grad_inner_two = product_nt(grad_attn[prompt_rows:], up_attention_out).astype(jnp.bfloat16)
    grad_context = product_nt(grad_attn, frozen_attention_out)
    grad_context = (
        grad_context.at[prompt_rows:]
        .add(product_nt(grad_inner_two, down_attention_out))
        .astype(jnp.bfloat16)
    )

    def backward_head(operands):
        query_head, key_head, value_head, grad_head, total_head = operands
        scores = jnp.where(allowed, product_nt(query_head, key_head) * 0.125, NEGATIVE)
        prob_full = jnp.exp(scores - total_head[:, None])
        weights = prob_full.astype(jnp.bfloat16)
        grad_weights = product_nt(grad_head, value_head)
        row_delta = jnp.sum(prob_full * grad_weights, axis=1, keepdims=True)
        grad_scores = (prob_full * (grad_weights - row_delta)).astype(jnp.bfloat16)
        return (
            product(grad_scores, key_head) * 0.125,
            product_tn(grad_scores, query_head) * 0.125,
            product_tn(weights, grad_head),
        )

    grad_q, grad_k, grad_v = lax.map(
        backward_head, (query_heads, key_heads, value_heads, split_heads(grad_context), log_total)
    )
    grad_query = merge_heads(grad_q)
    grad_keys = merge_heads(grad_k)
    grad_values = merge_heads(grad_v)
    own_keys, own_values = (
        lax.psum_scatter(
            grad_keys[:prompt_total].astype(jnp.bfloat16), "seq", scatter_dimension=0, tiled=True
        ).astype(jnp.float32),
        lax.psum_scatter(
            grad_values[:prompt_total].astype(jnp.bfloat16), "seq", scatter_dimension=0, tiled=True
        ).astype(jnp.float32),
    )
    grad_qkv = jnp.concatenate(
        [
            grad_query,
            jnp.concatenate([own_keys, grad_keys[prompt_total:]], 0),
            jnp.concatenate([own_values, grad_values[prompt_total:]], 0),
        ],
        1,
    ).astype(jnp.bfloat16)
    grad_inner_one = product_nt(grad_qkv[prompt_rows:], up_query_key_value).astype(jnp.bfloat16)
    grad_normed_one = product_nt(grad_qkv, frozen_query_key_value)
    grad_normed_one = grad_normed_one.at[prompt_rows:].add(
        product_nt(grad_inner_one, down_query_key_value)
    )
    first_pull = jax.vjp(lambda field: layer_norm(field, layer_norm_gains[0], shift_one), inputs)[1]
    input_grad = grad_hidden + first_pull(grad_normed_one)[0]
    down_term = jnp.concatenate(
        [
            product_tn(normed_one[prompt_rows:], grad_inner_one),
            product_tn(attention_context[prompt_rows:], grad_inner_two),
            product_tn(normed_two[prompt_rows:], grad_inner_three),
            product_tn(activated_hidden[prompt_rows:], grad_inner_four),
        ],
        0,
    )
    up_term = jnp.concatenate(
        [
            product_tn(inner_one, grad_qkv[prompt_rows:]),
            product_tn(inner_two, grad_attn[prompt_rows:]),
            product_tn(inner_three, grad_pre[prompt_rows:]),
            product_tn(inner_four, cotangent[prompt_rows:]),
        ],
        1,
    )
    select = (jnp.arange(ADAPTER_COUNT, dtype=jnp.int32) == adapter_index).astype(jnp.float32)
    down_grad, up_grad = (
        lax.psum_scatter(
            (select[:, None, None] * down_term[None]).reshape(-1),
            ("grp", "seq"),
            scatter_dimension=0,
            tiled=True,
        ),
        lax.psum_scatter(
            (select[:, None, None] * up_term[None]).reshape(-1),
            ("grp", "seq"),
            scatter_dimension=0,
            tiled=True,
        ),
    )
    return (outputs, input_grad, down_grad, up_grad)


def solution(mesh):
    placed = (
        P(("grp", "seq"), None),
        P(("grp", "seq"), None),
        P(("grp", "seq")),
        P(("grp", "seq")),
        P(("grp", "seq")),
        P(("grp", "seq")),
        P(),
        P(),
        P(("grp", "seq")),
        P(("grp", "seq")),
        P(("grp", "seq"), None),
    )
    return jax.shard_map(
        local,
        mesh=mesh,
        in_specs=placed,
        out_specs=(
            P(("grp", "seq"), None),
            P(("grp", "seq"), None),
            P(("grp", "seq")),
            P(("grp", "seq")),
        ),
        check_vma=False,
    )
```

profile of v0, /device:TPU:0, one launch (start us, length us, event | category | flops | bytes accessed | tf_op | source)
XLA Modules:
  0.0 1099.7 jit_solution(9629580832260513346)
XLA Ops:
  16.6 52.9 %all-gather.11.cloned.1.call-done = bf16[917504]{0:T(1024)(128)(2,1)} async-done(((bf16[28672]{0:T(1024)(128)(2,1)}), bf16[917504]{0:T(1024)(128)(2,1)}) %all-gather.11.cloned.1.call-update) | async-done | bytes 1835024 | tf_op jit(solution)/shard_map/all_gather | solution.py:118
  69.5 15.4 %reshape.374 = bf16[8,7168,16]{2,1,0:T(8,128)(2,1)} reshape(bf16[917504]{0:T(1024)(128)(2,1)} %all-gather.11.cloned.1.call-done) | data formatting | bytes 3670016 | tf_op jit(solution)/shard_map/reshape | solution.py:44
  86.2 42.3 %all-gather.13.cloned.1.call-done = bf16[1179648]{0:T(1024)(128)(2,1)} async-done(((bf16[36864]{0:T(1024)(128)(2,1)}), bf16[1179648]{0:T(1024)(128)(2,1)}) %all-gather.13.cloned.1.call-update) | async-done | bytes 2359312 | tf_op jit(solution)/shard_map/all_gather | solution.py:119
  128.5 4.3 reshape.375
  133.8 65.9 %all-gather.9.cloned.1.call-done = bf16[3145728]{0:T(1024)(128)(2,1)} async-done(((bf16[98304]{0:T(1024)(128)(2,1)}), bf16[3145728]{0:T(1024)(128)(2,1)}) %all-gather.9.cloned.1.call-update) | async-done | bytes 6291472 | tf_op jit(solution)/shard_map/all_gather | solution.py:114
  199.7 10.3 reshape.373
  210.0 6.3 convolution_add_fusion.1
  223.4 34.1 %all-gather.19.cloned.1.call-done = bf16[1048576]{0:T(1024)(128)(2,1)} async-done(((bf16[32768]{0:T(1024)(128)(2,1)}), bf16[1048576]{0:T(1024)(128)(2,1)}) %all-gather.19.cloned.1.call-update) | async-done | bytes 2097168 | tf_op jit(solution)/shard_map/all_gather | solution.py:115
  257.4 4.2 reshape.379
  268.6 18.3 %all-gather.15.cloned.1.call-done = bf16[1024,1024]{1,0:T(8,128)(2,1)} async-done(((bf16[128,1024]{1,0:T(8,128)(2,1)}), bf16[1024,1024]{1,0:T(8,128)(2,1)}) %all-gather.15.cloned.1.call-update) | async-done | bytes 2097168 | tf_op jit(solution)/shard_map/all_gather | solution.py:156
  286.9 30.0 %all-gather.17.cloned.1.call-done = bf16[1024,1024]{1,0:T(8,128)(2,1)} async-done(((bf16[128,1024]{1,0:T(8,128)(2,1)}), bf16[1024,1024]{1,0:T(8,128)(2,1)}) %all-gather.17.cloned.1.call-update) | async-done | bytes 2097168 | tf_op jit(solution)/shard_map/all_gather | solution.py:159
  317.0 4.4 pad_maximum_fusion
  321.4 4.7 copy.33
  326.1 6.7 copy.36
  335.7 6.6 copy.37
  342.5 160.8 %while.36 = (s32[]{:T(128)}, bf16[16,640,64]{1,2,0:T(8,128)(2,1)S(1)}, f32[16,640]{1,0:T(8,128)}, bf16[16,640,64]{2,1,0:T(8,128)(2,1)}, bf16[16,1536,64]{2,1,0:T...) while((s32[]{:T(128)}, ...), condition=%wide.region_5.6_spmd.clone, body=%wide.region_2.0_spmd.clone.sunk | while | flops 264437120 | bytes 28688668 | solution.py:179
  511.9 13.3 %reshape.381 = bf16[4096,1024]{1,0:T(8,128)(2,1)} reshape(bf16[4194304]{0:T(1024)(128)(2,1)} %all-gather.23.cloned.1.call-done) | data formatting | bytes 16777216 | tf_op jit(solution)/shard_map/reshape | solution.py:54
  525.2 12.2 %fusion.134 = f32[640,4096]{1,0:T(8,128)} fusion(bf16[640,1024]{1,0:T(8,128)(2,1)} %param.32, bf16[4096,1024]{1,0:T(8,128)(2,1)} %reshape.381), kind=kOutput, calls=%fused_computation.202 | convolution fusion | flops 5368709120 | bytes 20185088 | tf_op jit(solution)/shard_map/dot_general | solution.py:30
  537.5 13.3 %reshape.380 = bf16[1024,4096]{1,0:T(8,128)(2,1)} reshape(bf16[4194304]{0:T(1024)(128)(2,1)} %all-gather.21.cloned.1.call-done) | data formatting | bytes 16777216 | tf_op jit(solution)/shard_map/reshape | solution.py:53
  550.8 8.5 convolution_add_fusion
  563.8 8.6 fusion.52
  572.5 5.3 fusion.92
  578.1 8.8 fusion.135
  589.4 5.6 convolution_add_fusion.2
  606.9 182.3 %while.37 = (s32[]{:T(128)}, bf16[16,640,64]{1,2,0:T(8,128)(2,1)S(1)}, bf16[16,1536,64]{1,2,0:T(8,128)(2,1)}, bf16[16,1536,64]{1,2,0:T(8,128)(2,1)}, bf16[16,640...) while((s32[]{:T(128)}, ...), condition=%wide.region_12.13_spmd.clone, body=%wide.region_10.12_spmd.clone.sunk | while | flops 643046784 | bytes 32144144 | solution.py:257
  811.5 18.9 %reduce-scatter.7.cloned.1.call-done = bf16[128,1024]{1,0:T(8,128)(2,1)} async-done(((bf16[1024,1024]{1,0:T(8,128)(2,1)}), bf16[128,1024]{1,0:T(8,128)(2,1)}) %reduce-scatter.7.cloned.1.call-update) | async-done | bytes 262160
  831.6 36.4 %reduce-scatter.9.cloned.1.call-done = bf16[128,1024]{1,0:T(8,128)(2,1)} async-done(((bf16[1024,1024]{1,0:T(8,128)(2,1)}), bf16[128,1024]{1,0:T(8,128)(2,1)}) %reduce-scatter.9.cloned.1.call-update) | async-done | bytes 262160
  869.1 4.1 maximum_maximum_fusion
  881.9 11.1 %broadcast_multiply_fusion = f32[8,7168,16]{2,1,0:T(8,128)} fusion(f32[7168,16]{1,0:T(8,128)} %copy.43, f32[8]{0:T(128)S(1)} %copy-done.52), kind=kLoop, calls=%fused_computation.59 | loop fusion | flops 917504 | bytes 4128800 | tf_op jit(solution)/shard_map/mul | solution.py:307
  893.0 18.8 %mul.251 = f32[917504]{0:T(1024)} reshape(f32[8,7168,16]{2,1,0:T(8,128)} %broadcast_multiply_fusion) | data formatting | bytes 7340032 | tf_op jit(solution)/shard_map/mul | solution.py:307
  913.1 8.0 fusion.56
  926.9 162.7 %all-reduce.5.cloned.1.call-done = (f32[917504]{0:T(1024)}, f32[1179648]{0:T(1024)}) async-done(((f32[917504]{0:T(1024)}, f32[1179648]{0:T(1024)}), (f32[917504]{0:T(1024)}, f32[1179648]{0:T(1024)})) %all-reduce.5.cloned.1.call-update) | async-done | bytes 8388624
  (473 shorter events, 440.4 us)
Async XLA Ops:
  7.2 8.9 copy-start.1
  7.2 8.8 copy-start.49
  7.2 62.3 %all-gather.11.cloned.1.call-start = ((), (), s32[]{:S(2)}) async-start(), calls=%async_computation.3 | async-start | bytes 1892352 | tf_op jit(solution)/shard_map/all_gather | solution.py:118
  7.9 120.6 %all-gather.13.cloned.1.call-start = ((), (), s32[]{:S(2)}) async-start(), calls=%async_computation.4 | async-start | bytes 2433024 | tf_op jit(solution)/shard_map/all_gather | solution.py:119
  8.7 191.0 %all-gather.9.cloned.1.call-start = ((), (), s32[]{:S(2)}) async-start(), calls=%async_computation.2 | async-start | bytes 6488064 | tf_op jit(solution)/shard_map/all_gather | solution.py:114
  9.4 248.0 %all-gather.19.cloned.1.call-start = ((), (), s32[]{:S(2)}) async-start(), calls=%async_computation.7 | async-start | bytes 2162688 | tf_op jit(solution)/shard_map/all_gather | solution.py:115
  10.0 276.9 %all-gather.15.cloned.1.call-start = ((), (), s32[]{:S(2)}) async-start(), calls=%async_computation.5 | async-start | bytes 2359296 | tf_op jit(solution)/shard_map/all_gather | solution.py:156
  12.2 57.2 %copy-start.37 = (f32[640]{0:T(1024)}, f32[640]{0:T(1024)S(1)}, u32[]{:S(2)}) copy-start(f32[640]{0:T(1024)S(1)} %broadcast_multiply_fusion.3) | copy-start | bytes 7684
  16.0 53.5 %copy-start.43 = (f32[640]{0:T(1024)}, f32[640]{0:T(1024)S(1)}, u32[]{:S(2)}) copy-start(f32[640]{0:T(1024)S(1)} %fusion.115) | copy-start | bytes 7684
  16.0 53.4 %copy-start.39 = (f32[1,1024]{1,0:T(1,128)}, f32[1,1024]{1,0:T(1,128)S(1)}, u32[]{:S(2)}) copy-start(f32[1,1024]{1,0:T(1,128)S(1)} %get-tuple-element.385) | copy-start | bytes 12292
  16.6 193.4 %copy-start.14 = (bf16[640,1024]{1,0:T(8,128)(2,1)}, bf16[640,1024]{1,0:T(8,128)(2,1)S(1)}, u32[]{:S(2)}) copy-start(bf16[640,1024]{1,0:T(8,128)(2,1)S(1)} %fusion.81) | copy-start | bytes 3932164
  86.2 130.1 %copy-start.31 = (bf16[512,16]{0,1:T(8,128)(2,1)}, bf16[512,16]{0,1:T(8,128)(2,1)S(1)}, u32[]{:S(2)}) copy-start(bf16[512,16]{0,1:T(8,128)(2,1)S(1)} %convolution_convert_fusion.5) | copy-start | bytes 49156
  133.8 466.4 %copy-start.24 = (bf16[16,9216]{1,0:T(8,128)(2,1)}, bf16[16,9216]{1,0:T(8,128)(2,1)S(1)}, u32[]{:S(2)}) copy-start(bf16[16,9216]{1,0:T(8,128)(2,1)S(1)} %dynamic-slice_bitcast_fusion.3) | copy-start | bytes 884740
  220.1 41.5 %copy-start.7 = (bf16[640,1024]{1,0:T(8,128)(2,1)S(1)}, bf16[640,1024]{1,0:T(8,128)(2,1)}, u32[]{:S(2)}) copy-start(bf16[640,1024]{1,0:T(8,128)(2,1)} %param.32) | copy-start | bytes 3932164
  220.9 96.0 %all-gather.17.cloned.1.call-start = ((), (), s32[]{:S(2)}) async-start(), calls=%async_computation.6 | async-start | bytes 2359296 | tf_op jit(solution)/shard_map/all_gather | solution.py:159
  221.5 290.4 %all-gather.23.cloned.1.call-start = ((), (), s32[]{:S(2)}) async-start(), calls=%async_computation.9 | async-start | bytes 8650752 | tf_op jit(solution)/shard_map/all_gather | solution.py:117
  222.3 315.2 %all-gather.21.cloned.1.call-start = ((), (), s32[]{:S(2)}) async-start(), calls=%async_computation.8 | async-start | bytes 8650752 | tf_op jit(solution)/shard_map/all_gather | solution.py:116
  223.0 607.4 %reduce-scatter.7.cloned.1.call-start = ((), (), s32[]{:S(2)}) async-start(), calls=%async_computation.10 | async-start | bytes 2359296
  511.9 47.4 %copy-start.35 = (bf16[512,16]{0,1:T(8,128)(2,1)}, bf16[512,16]{0,1:T(8,128)(2,1)S(1)}, u32[]{:S(2)}) copy-start(bf16[512,16]{0,1:T(8,128)(2,1)S(1)} %convolution_convert_fusion.3) | copy-start | bytes 49156
  537.5 13.3 %slice-start.8 = ((f32[10240]{0:T(1024)}), f32[4096]{0:T(1024)S(1)}, s32[]{:S(2)}) async-start(f32[10240]{0:T(1024)} %param.38), calls=%async_computation.21 | async-start | bytes 32768 | tf_op jit(solution)/shard_map/slice | solution.py:146
  550.8 10.1 slice-start
  550.8 10.1 slice-start.1
  572.4 16.9 %copy-start.4 = (bf16[640,4096]{1,0:T(8,128)(2,1)}, bf16[640,4096]{1,0:T(8,128)(2,1)S(1)}, u32[]{:S(2)}) copy-start(bf16[640,4096]{1,0:T(8,128)(2,1)S(1)} %get-tuple-element.372) | copy-start | bytes 15728644
  572.5 16.9 %slice-start.6 = ((s8[8388608]{0:T(1024)(128)(4,1)}), s8[4194304]{0:T(1024)(128)(4,1)S(1)}, s32[]{:S(2)}) async-start(s8[8388608]{0:T(1024)(128)(4,1)} %bitcast.192), calls=%async_computation.19 | async-start | bytes 8388608
  578.1 17.0 %copy-start.41 = (bf16[512,16]{0,1:T(8,128)(2,1)}, bf16[512,16]{0,1:T(8,128)(2,1)S(1)}, u32[]{:S(2)}) copy-start(bf16[512,16]{0,1:T(8,128)(2,1)S(1)} %fusion.92) | copy-start | bytes 49156
  578.1 11.3 %slice-start.7 = ((s8[8388608]{0:T(1024)(128)(4,1)}), s8[4194304]{0:T(1024)(128)(4,1)S(1)}, s32[]{:S(2)}) async-start(s8[8388608]{0:T(1024)(128)(4,1)} %bitcast.192), calls=%async_computation.20 | async-start | bytes 8388608
  794.8 73.1 %reduce-scatter.9.cloned.1.call-start = ((), (), s32[]{:S(2)}) async-start(), calls=%async_computation.11 | async-start | bytes 2359296
  796.7 13.4 %slice-start.3 = ((s8[5242880]{0:T(1024)(128)(4,1)}), s8[1048576]{0:T(1024)(128)(4,1)S(1)}, s32[]{:S(2)}) async-start(s8[5242880]{0:T(1024)(128)(4,1)} %bitcast.182), calls=%async_computation.16 | async-start | bytes 2097152
  799.3 290.2 %all-reduce.5.cloned.1.call-start = ((), (), s32[]{:S(2)}) async-start(), calls=%async_computation.12 | async-start | bytes 16777216
  800.0 6.5 copy-start.36
  801.6 8.5 slice-start.4
  831.6 41.7 %copy-start.25 = (bf16[128,1024]{0,1:T(8,128)(2,1)}, bf16[128,1024]{0,1:T(8,128)(2,1)S(1)}, u32[]{:S(2)}) copy-start(bf16[128,1024]{0,1:T(8,128)(2,1)S(1)} %copy.45) | copy-start | bytes 786436
  (56 other events, 143.2 us)
Sparse Core Ops, SparseCore 0:
  10.9 58.5 all-gather.10
  72.5 55.9 all-gather.12
  131.5 68.1 all-gather.8
  202.5 54.8 all-gather.18
  258.9 27.9 all-gather.14
  288.4 28.5 all-gather.16
  319.9 76.4 all-gather.22
  399.4 75.6 all-gather.20
  794.9 35.4 reduce-scatter.6
  833.2 34.7 reduce-scatter.8
  912.0 177.5 all-reduce.4
where the time goes:
time: 1110 us; the launch traced here: 1100 us
  waiting for transfers between devices  466 us (42%)
  matrix products  347 us (31%)
  local copies, waits for them, and re-layouts  210 us (19%)
  other arithmetic  59.6 us (5%)
  between operations  15.9 us (1%)
    unnamed x14, waiting for transfers between devices  223 us
    dot_general x60, matrix products, product_nt(): lax.dot_general(left_side, right_side, (((1,), (1,)), ((), ())), preferre...  176 us
    dot_general x44, matrix products, product(): return jnp.dot(left_side, right_side, preferred_element_type=jnp.float32)  110 us
    all_gather x1, waiting for transfers between devices, local(): lax.all_gather(weight_shards[0], ('grp', 'seq'), axis=0, tiled=True)  65.9 us
    dot_general x40, matrix products, product_tn(): lax.dot_general(left_side, right_side, (((0,), (0,)), ((), ())), preferre...  60.9 us
    all_gather x1, waiting for transfers between devices, local(): lax.all_gather(weight_shards[4], ('grp', 'seq'), axis=0, tiled=True)  52.9 us
    all_gather x1, waiting for transfers between devices, local(): lax.all_gather(weight_shards[5], ('grp', 'seq'), axis=0, tiled=True)  42.3 us
    unnamed x128, local copies, waits for them, and re-layouts  39.4 us
  transfers between devices with their start and end apart: 11, of which 9 were waited for; matrix products, arithmetic and copies ran while one was open for 25% of the time, Pallas kernels for 0%

commit v1 on v0

--- a/solution.py
+++ b/solution.py
@@ -1,6 +1,10 @@
+import functools
+
 import jax
 import jax.numpy as jnp
 from jax import lax
+from jax.experimental import pallas as pl
+from jax.experimental.pallas import tpu as pltpu
 from jax.sharding import PartitionSpec as P
 
 MODEL_WIDTH = 1024
@@ -83,7 +87,627 @@
     return values.transpose(1, 0, 2).reshape(values.shape[1], HEADS * HEAD_DIM)
 
 
-def local(
+MESH = pl.DeviceIdType.MESH
+SCALE2 = 0.125 * 1.4426950408889634
+VMEM_LIMIT = 60 << 20
+
+
+def gather_stages(groups, sizes, chunks, ins, outs, sems):
+    grp_n, seq_n = groups
+    z_n, y_n = seq_n // 2, grp_n // 2
+    z_sem, x_sem, y_sem, d_sem, p_sem, s_sem, l_sem = sems
+    g, s = lax.axis_index("grp"), lax.axis_index("seq")
+    core, z = lax.rem(s, 2), s // 2
+    gx, gy = lax.rem(g, 2), g // 2
+    partner = (g, z * 2 + 1 - core)
+    other_x = gy * 2 + 1 - gx
+    x_next = (other_x, s)
+    far_z = [lax.rem(z + d, z_n) for d in range(1, z_n)]
+    far_y = [lax.rem(gy + d, y_n) for d in range(1, y_n)]
+    y_next = [(y * 2 + gx, s) for y in far_y]
+
+    def enter():
+        peers = [partner, x_next] + y_next + [(g, far * 2 + core) for far in far_z]
+        barrier = pltpu.get_barrier_semaphore()
+        for peer in peers:
+            pl.semaphore_signal(barrier, inc=1, device_id=peer, device_id_type=MESH)
+        pl.semaphore_wait(barrier, len(peers))
+
+    def place(ch, gg, ss):
+        arr, row, rows, full = chunks[ch]
+        block = gg * seq_n + ss if full else ss
+        return outs[arr].at[pl.ds(pl.multiple_of(block * sizes[arr] + row, 16), rows)]
+
+    def send(ch, src, gg, ss, sem, device):
+        pltpu.make_async_remote_copy(
+            src_ref=src,
+            dst_ref=place(ch, gg, ss),
+            send_sem=s_sem.at[ch],
+            recv_sem=sem,
+            device_id=device,
+            device_id_type=MESH,
+        ).start()
+
+    def drain(ch, sem, count=1):
+        arr, _, rows, _ = chunks[ch]
+        block = outs[arr].at[pl.ds(0, count * rows)]
+        pltpu.make_async_copy(block, block, sem).wait()
+
+    def own(ch):
+        arr, row, rows, full = chunks[ch]
+        src = ins[arr].at[pl.ds(row, rows)]
+        for far in far_z:
+            send(ch, src, g, s, z_sem.at[ch, z], (g, far * 2 + core))
+        if full:
+            send(ch, src, g, s, x_sem.at[ch, z], x_next)
+            for peer in y_next:
+                send(ch, src, g, s, y_sem.at[ch, gy, z], peer)
+        send(ch, src, g, s, p_sem.at[ch], partner)
+        pltpu.make_async_copy(src, place(ch, g, s), l_sem.at[ch]).start()
+
+    def line(ch):
+        for far in far_z:
+            drain(ch, z_sem.at[ch, far])
+            from_s = far * 2 + core
+            src = place(ch, g, from_s)
+            if chunks[ch][3]:
+                send(ch, src, g, from_s, x_sem.at[ch, far], x_next)
+                for peer in y_next:
+                    send(ch, src, g, from_s, y_sem.at[ch, gy, far], peer)
+            send(ch, src, g, from_s, p_sem.at[ch], partner)
+
+    def side(ch):
+        if not chunks[ch][3]:
+            return
+        for far in range(z_n):
+            from_s = far * 2 + core
+            drain(ch, x_sem.at[ch, far])
+            src = place(ch, other_x, from_s)
+            if far % 2 == 0:
+                for peer in y_next:
+                    send(ch, src, other_x, from_s, d_sem.at[ch, gy, far], peer)
+            send(ch, src, other_x, from_s, p_sem.at[ch], partner)
+            for y in far_y:
+                drain(ch, y_sem.at[ch, y, far])
+                from_g = y * 2 + gx
+                src = place(ch, from_g, from_s)
+                if far % 2 == 1:
+                    send(ch, src, from_g, from_s, d_sem.at[ch, y, far], x_next)
+                send(ch, src, from_g, from_s, p_sem.at[ch], partner)
+
+    def corner(ch):
+        if not chunks[ch][3]:
+            return
+        for far in range(z_n):
+            from_s = far * 2 + core
+            for y in far_y:
+                drain(ch, d_sem.at[ch, y, far])
+                from_g = y * 2 + 1 - gx
+                src = place(ch, from_g, from_s)
+                send(ch, src, from_g, from_s, p_sem.at[ch], partner)
+
+    def finish(ch):
+        blocks, sends = z_n, 2 * z_n - 1
+        if chunks[ch][3]:
+            blocks = z_n * grp_n
+            sends += z_n * y_n
+            sends += z_n * (y_n - 1)
+            sends += z_n * (2 * y_n - 1)
+        drain(ch, p_sem.at[ch], blocks)
+        drain(ch, s_sem.at[ch], sends)
+        drain(ch, l_sem.at[ch])
+
+    steps = (own, line, side, corner)
+
+    def tick(t):
+        for lag, step in enumerate(steps):
+            if 0 <= t - lag < len(chunks):
+                step(t - lag)
+
+    def close():
+        for ch in range(len(chunks)):
+            finish(ch)
+
+    return enter, tick, close, len(chunks) + len(steps) - 1
+
+
+def gather_plan(groups, arrays, fulls, splits):
+    grp_n, seq_n = groups
+    chunks = []
+    for i, array in enumerate(arrays):
+        rows = array.shape[0] // splits[i]
+        chunks += [(i, j * rows, rows, fulls[i]) for j in range(splits[i])]
+    shapes = [
+        jax.ShapeDtypeStruct(((grp_n if full else 1) * seq_n * a.shape[0], a.shape[1]), a.dtype)
+        for a, full in zip(arrays, fulls)
+    ]
+    dma, count = pltpu.SemaphoreType.DMA, len(chunks)
+    sems = [
+        dma((count, seq_n // 2)),
+        dma((count, seq_n // 2)),
+        dma((count, grp_n // 2, seq_n // 2)),
+        dma((count, grp_n // 2, seq_n // 2)),
+        dma((count,)),
+        dma((count,)),
+        dma((count,)),
+    ]
+    return [a.shape[0] for a in arrays], chunks, shapes, sems
+
+
+def gather_arrays(groups, arrays, fulls, splits, collective_id):
+    sizes, chunks, shapes, sems = gather_plan(groups, arrays, fulls, splits)
+    count = len(arrays)
+
+    def kernel(*refs):
+        enter, tick, close, ticks = gather_stages(
+            groups, sizes, chunks, refs[:count], refs[count : 2 * count], refs[2 * count :]
+        )
+        enter()
+        for t in range(ticks):
+            tick(t)
+        close()
+
+    return pl.pallas_call(
+        kernel,
+        out_shape=shapes,
+        in_specs=[pl.BlockSpec(memory_space=pltpu.VMEM)] * count,
+        out_specs=[pl.BlockSpec(memory_space=pl.ANY)] * count,
+        scratch_shapes=sems,
+        compiler_params=pltpu.CompilerParams(collective_id=collective_id, has_side_effects=True),
+    )(*arrays)
+
+
+def dot_nt(left, right):
+    return lax.dot_general(
+        left, right, (((1,), (1,)), ((), ())), preferred_element_type=jnp.float32
+    )
+
+
+def dot_nn(left, right):
+    return lax.dot_general(
+        left, right, (((1,), (0,)), ((), ())), preferred_element_type=jnp.float32
+    )
+
+
+def stacked_heads(pair):
+    first = lax.broadcasted_iota(jnp.int32, pair.shape, 1) < HEAD_DIM
+    zero = jnp.zeros_like(pair)
+    return jnp.concatenate([jnp.where(first, pair, zero), jnp.where(first, zero, pair)], 0)
+
+
+def row_groups(prompt_rows, prompt_total, later_rows):
+    block = min(256, later_rows)
+    return [(prompt_rows + i, block, prompt_total + i) for i in range(0, later_rows, block)]
+
+
+def attention_forward(sizes, q_ref, k_ref, v_ref, ctx_ref, lse_ref, wide_ref):
+    prompt_rows, prompt_total, later_rows = sizes
+    seq = lax.axis_index("seq")
+    wide_ref[:, :128] = v_ref[...]
+    wide_ref[:, 128:] = jnp.ones((prompt_total + later_rows, 128), jnp.bfloat16)
+
+    def finish(start, rows, row_max, summed):
+        total = summed[:, 128:]
+        mixed = summed[:, :128] / total
+        log_total = row_max * SCALE2 + jnp.log2(total)
+        first = lax.broadcasted_iota(jnp.int32, (rows, 128), 1) < HEAD_DIM
+        ctx_ref[start : start + rows] = jnp.where(first, mixed[:rows], mixed[rows:]).astype(
+            jnp.bfloat16
+        )
+        lse_ref[start : start + rows] = jnp.where(first, log_total[:rows], log_total[rows:])
+
+    for start, rows, free in row_groups(prompt_rows, prompt_total, later_rows):
+        queries = stacked_heads(q_ref[start : start + rows])
+        open_scores = dot_nt(queries, k_ref[:free])
+        edge_scores = dot_nt(queries, k_ref[free : free + rows])
+        row = lax.broadcasted_iota(jnp.int32, (rows, rows), 0)
+        key = lax.broadcasted_iota(jnp.int32, (rows, rows), 1)
+        seen = key <= row
+        edge_scores = jnp.where(jnp.concatenate([seen, seen], 0), edge_scores, NEGATIVE)
+        row_max = jnp.maximum(
+            jnp.max(open_scores, 1, keepdims=True), jnp.max(edge_scores, 1, keepdims=True)
+        )
+        scaled = row_max * SCALE2
+        open_p = jnp.exp2(open_scores * SCALE2 - scaled).astype(jnp.bfloat16)
+        edge_p = jnp.exp2(edge_scores * SCALE2 - scaled).astype(jnp.bfloat16)
+        summed = dot_nn(open_p, wide_ref[:free]) + dot_nn(edge_p, wide_ref[free : free + rows])
+        finish(start, rows, row_max, summed)
+    scores = dot_nt(stacked_heads(q_ref[:prompt_rows]), k_ref[:prompt_total])
+    row = lax.broadcasted_iota(jnp.int32, (prompt_rows, prompt_total), 0)
+    key = lax.broadcasted_iota(jnp.int32, (prompt_rows, prompt_total), 1)
+    seen = key <= row + seq * prompt_rows
+    scores = jnp.where(jnp.concatenate([seen, seen], 0), scores, NEGATIVE)
+    row_max = jnp.max(scores, 1, keepdims=True)
+    p = jnp.exp2(scores * SCALE2 - row_max * SCALE2).astype(jnp.bfloat16)
+    finish(0, prompt_rows, row_max, dot_nn(p, wide_ref[:prompt_total]))
+
+
+def attention_backward(
+    sizes, q_ref, k_ref, v_ref, d_ref, ctx_ref, lse_ref, dq_ref, dk_ref, dv_ref, k_sum, v_sum
+):
+    prompt_rows, prompt_total, later_rows = sizes
+    seq = lax.axis_index("seq")
+    keys_t = k_ref[...].astype(jnp.float32).T.astype(jnp.bfloat16)
+    lse_t = lse_ref[...].T
+    weighed_t = (d_ref[...].astype(jnp.float32) * ctx_ref[...].astype(jnp.float32)).T
+    deltas = [
+        jnp.sum(weighed_t[:HEAD_DIM], 0, keepdims=True),
+        jnp.sum(weighed_t[HEAD_DIM:], 0, keepdims=True),
+    ]
+    totals = [lse_t[0:1], lse_t[HEAD_DIM : HEAD_DIM + 1]]
+
+    def group(start, rows, count, mask):
+        queries = stacked_heads(q_ref[start : start + rows])
+        grads = stacked_heads(d_ref[start : start + rows])
+        total = jnp.concatenate([t[:, start : start + rows] for t in totals], 1)
+        delta = jnp.concatenate([t[:, start : start + rows] for t in deltas], 1)
+        p = mask(jnp.exp2(dot_nt(k_ref[:count], queries) * SCALE2 - total))
+        d_scores = (p * (dot_nt(v_ref[:count], grads) - delta)).astype(jnp.bfloat16)
+        dq_t = dot_nn(keys_t[:, :count], d_scores)
+        first = lax.broadcasted_iota(jnp.int32, (128, rows), 0) < HEAD_DIM
+        dq = jnp.where(first, dq_t[:, :rows], dq_t[:, rows:]).T * 0.125
+        dq_ref[start : start + rows] = dq.astype(jnp.bfloat16)
+        return dot_nn(d_scores, queries), dot_nn(p.astype(jnp.bfloat16), grads)
+
+    def causal(free, rows):
+        def mask(p):
+            key = lax.broadcasted_iota(jnp.int32, (rows, rows), 0)
+            row = lax.broadcasted_iota(jnp.int32, (rows, rows), 1)
+            seen = key <= row
+            edge = jnp.where(jnp.concatenate([seen, seen], 1), p[free:], 0.0)
+            return jnp.concatenate([p[:free], edge], 0)
+
+        return mask
+
+    def prompt_mask(p):
+        key = lax.broadcasted_iota(jnp.int32, (prompt_total, prompt_rows), 0)
+        row = lax.broadcasted_iota(jnp.int32, (prompt_total, prompt_rows), 1)
+        seen = key <= row + seq * prompt_rows
+        return jnp.where(jnp.concatenate([seen, seen], 1), p, 0.0)
+
+    groups = row_groups(prompt_rows, prompt_total, later_rows)
+    start, rows, free = groups[-1]
+    k_sum[...], v_sum[...] = group(start, rows, free + rows, causal(free, rows))
+    for start, rows, free in groups[:-1]:
+        d_keys, d_values = group(start, rows, free + rows, causal(free, rows))
+        k_sum[: free + rows] += d_keys
+        v_sum[: free + rows] += d_values
+    d_keys, d_values = group(0, prompt_rows, prompt_total, prompt_mask)
+    k_sum[:prompt_total] += d_keys
+    v_sum[:prompt_total] += d_values
+    dk_ref[...] = (k_sum[...] * 0.125).astype(jnp.bfloat16)
+    dv_ref[...] = v_sum[...].astype(jnp.bfloat16)
+
+
+def attend_and_gather(groups, q, kv, arrays, splits, collective_id):
+    rows, keys, pairs = q.shape[0], kv.shape[0], q.shape[1] // 128
+    sizes = (rows - CONT_LEN, keys - CONT_LEN, CONT_LEN)
+    lengths, chunks, shapes, sems = gather_plan(groups, arrays, [True] * len(arrays), splits)
+    count = len(arrays)
+
+    def kernel(q_ref, k_ref, v_ref, *refs):
+        ins, refs = refs[:count], refs[count:]
+        ctx_ref, lse_ref, outs, wide_ref, sem_refs = (
+            refs[0],
+            refs[1],
+            refs[2 : 2 + count],
+            refs[2 + count],
+            refs[3 + count :],
+        )
+        enter, tick, close, ticks = gather_stages(groups, lengths, chunks, ins, outs, sem_refs)
+        step = pl.program_id(0)
+        for i in range(pairs):
+
+            @pl.when(step == i)
+            def _():
+                if i == 0:
+                    enter()
+                if i < ticks:
+                    tick(i)
+
+        attention_forward(sizes, q_ref, k_ref, v_ref, ctx_ref, lse_ref, wide_ref)
+
+        @pl.when(step == pairs - 1)
+        def _():
+            for t in range(pairs, ticks):
+                tick(t)
+            close()
+
+    def pair(i):
+        return (0, i)
+
+    return pl.pallas_call(
+        kernel,
+        grid=(pairs,),
+        in_specs=[
+            pl.BlockSpec((rows, 128), pair),
+            pl.BlockSpec((keys, 128), pair),
+            pl.BlockSpec((keys, 128), lambda i: (0, pairs + i)),
+        ]
+        + [pl.BlockSpec(memory_space=pltpu.VMEM)] * count,
+        out_specs=[pl.BlockSpec((rows, 128), pair)] * 2
+        + [pl.BlockSpec(memory_space=pl.ANY)] * count,
+        out_shape=[
+            jax.ShapeDtypeStruct(q.shape, jnp.bfloat16),
+            jax.ShapeDtypeStruct(q.shape, jnp.float32),
+        ]
+        + shapes,
+        scratch_shapes=[pltpu.VMEM((keys, 256), jnp.bfloat16)] + sems,
+        compiler_params=pltpu.CompilerParams(
+            collective_id=collective_id, has_side_effects=True, vmem_limit_bytes=VMEM_LIMIT
+        ),
+    )(q, kv, kv, *arrays)
+
+
+def adapter_scratch(rows):
+    dma = pltpu.SemaphoreType.DMA
+    return [
+        pltpu.VMEM((2, rows, 128), jnp.bfloat16),
+        pltpu.VMEM((16, 128), jnp.bfloat16),
+        pltpu.VMEM((3, 4, rows, 128), jnp.bfloat16),
+        pltpu.VMEM((3, 4, rows, 128), jnp.bfloat16),
+        pltpu.VMEM((4, rows, 128), jnp.float32),
+        pltpu.VMEM((3, rows, 128), jnp.bfloat16),
+        pltpu.VMEM((3, rows, 128), jnp.bfloat16),
+        dma((3,)),
+        dma((3,)),
+        dma((3,)),
+        dma((3,)),
+        dma((3,)),
+        dma((3,)),
+    ]
+
+
+def adapter_stages(term_ref, id_ref, out_ref, scratch):
+    from_core, other_id, to_grp, from_grp, total, to_z, from_z = scratch[:7]
+    a_send, a_recv, g_send, g_recv, z_send, z_recv = scratch[7:]
+    g, s = lax.axis_index("grp"), lax.axis_index("seq")
+    core, z = lax.rem(s, 2), s // 2
+    other = 1 - core
+    partner = (g, z * 2 + other)
+    grps = [lax.rem(g + d, 4) for d in range(1, 4)]
+    lines = [lax.rem(z + d, 4) for d in range(1, 4)]
+
+    def enter():
+        peers = [partner] + [(far, s) for far in grps] + [(g, far * 2 + core) for far in lines]
+        barrier = pltpu.get_barrier_semaphore()
+        for peer in peers:
+            pl.semaphore_signal(barrier, inc=1, device_id=peer, device_id_type=MESH)
+        pl.semaphore_wait(barrier, len(peers))
+
+    def remote(src, dst, send_sem, recv_sem, device):
+        return pltpu.make_async_remote_copy(
+            src_ref=src,
+            dst_ref=dst,
+            send_sem=send_sem,
+            recv_sem=recv_sem,
+            device_id=device,
+            device_id_type=MESH,
+        )
+
+    copies_a = [
+        remote(term_ref.at[i * 2 + other], from_core.at[i], a_send.at[i], a_recv.at[i], partner)
+        for i in range(2)
+    ] + [remote(id_ref, other_id, a_send.at[2], a_recv.at[2], partner)]
+    copies_g = [
+        remote(to_grp.at[d], from_grp.at[d], g_send.at[d], g_recv.at[d], (grps[d], s))
+        for d in range(3)
+    ]
+    copies_z = [
+        remote(to_z.at[d], from_z.at[d], z_send.at[d], z_recv.at[d], (g, lines[d] * 2 + core))
+        for d in range(3)
+    ]
+
+    def start(copies):
+        for copy in copies:
+            copy.start()
+
+    def wait(copies):
+        for copy in copies:
+            copy.wait()
+
+    def select():
+        wait(copies_a)
+        mine = id_ref[0:1].astype(jnp.float32)
+        theirs = other_id[0:1].astype(jnp.float32)
+        for d, grp in enumerate(grps + [g]):
+            for slot in range(4):
+                adapter = (grp * 2 + slot // 2).astype(jnp.float32)
+                own_term = term_ref[(slot % 2) * 2 + core].astype(jnp.float32)
+                other_term = from_core[slot % 2].astype(jnp.float32)
+                picked = jnp.where(mine == adapter, own_term, 0.0) + jnp.where(
+                    theirs == adapter, other_term, 0.0
+                )
+                if d < 3:
+                    to_grp[d, slot] = picked.astype(jnp.bfloat16)
+                else:
+                    total[slot] = picked
+
+    def add_grps():
+        wait(copies_g)
+        for slot in range(4):
+            total[slot] += sum(from_grp[d, slot].astype(jnp.float32) for d in range(3))
+        for d in range(3):
+            to_z[d] = total[lines[d]].astype(jnp.bfloat16)
+
+    def add_lines():
+        wait(copies_z)
+        out_ref[...] = total[z] + sum(from_z[d].astype(jnp.float32) for d in range(3))
+
+    return (
+        enter,
+        lambda: start(copies_a),
+        select,
+        lambda: start(copies_g),
+        add_grps,
+        lambda: start(copies_z),
+        add_lines,
+    )
+
+
+def attend_back_and_reduce(q, kv, d_ctx, ctx, lse, term, ident, collective_id):
+    rows, keys, pairs = q.shape[0], kv.shape[0], q.shape[1] // 128
+    sizes = (rows - CONT_LEN, keys - CONT_LEN, CONT_LEN)
+    term_rows = term.shape[1]
+
+    def kernel(q_ref, k_ref, v_ref, d_ref, ctx_ref, lse_ref, term_ref, id_ref, *refs):
+        dq_ref, dk_ref, dv_ref, out_ref, k_sum, v_sum = refs[:6]
+        enter, send_core, select, send_grp, add_grps, send_z, add_lines = adapter_stages(
+            term_ref, id_ref, out_ref, refs[6:]
+        )
+        step = pl.program_id(0)
+
+        @pl.when(step == 0)
+        def _():
+            enter()
+            send_core()
+
+        @pl.when(step == 1)
+        def _():
+            select()
+
+        @pl.when(step == 2)
+        def _():
+            send_grp()
+
+        @pl.when(step == pairs - 2)
+        def _():
+            add_grps()
+
+        attention_backward(
+            sizes,
+            q_ref,
+            k_ref,
+            v_ref,
+            d_ref,
+            ctx_ref,
+            lse_ref,
+            dq_ref,
+            dk_ref,
+            dv_ref,
+            k_sum,
+            v_sum,
+        )
+
+        @pl.when(step == pairs - 2)
+        def _():
+            send_z()
+
+        @pl.when(step == pairs - 1)
+        def _():
+            add_lines()
+
+    def pair(i):
+        return (0, i)
+
+    row_spec = pl.BlockSpec((rows, 128), pair)
+    key_spec = pl.BlockSpec((keys, 128), pair)
+    whole = pl.BlockSpec(memory_space=pltpu.VMEM)
+    return pl.pallas_call(
+        kernel,
+        grid=(pairs,),
+        in_specs=[
+            row_spec,
+            key_spec,
+            pl.BlockSpec((keys, 128), lambda i: (0, pairs + i)),
+            row_spec,
+            row_spec,
+            row_spec,
+            whole,
+            whole,
+        ],
+        out_specs=[row_spec, key_spec, key_spec, whole],
+        out_shape=[
+            jax.ShapeDtypeStruct(q.shape, jnp.bfloat16),
+            jax.ShapeDtypeStruct((keys, q.shape[1]), jnp.bfloat16),
+            jax.ShapeDtypeStruct((keys, q.shape[1]), jnp.bfloat16),
+            jax.ShapeDtypeStruct((term_rows, 128), jnp.float32),
+        ],
+        scratch_shapes=[pltpu.VMEM((keys, 128), jnp.float32)] * 2 + adapter_scratch(term_rows),
+        compiler_params=pltpu.CompilerParams(
+            collective_id=collective_id, has_side_effects=True, vmem_limit_bytes=VMEM_LIMIT
+        ),
+    )(q, kv, kv, d_ctx, ctx, lse, term, ident)
+
+
+def last_exchange(rows_term, term, ident, collective_id):
+    blocks, cols = rows_term.shape[0], rows_term.shape[3]
+    rows = rows_term.shape[2]
+    term_rows = term.shape[1]
+    dma = pltpu.SemaphoreType.DMA
+
+    def kernel(x_ref, term_ref, id_ref, sum_ref, out_ref, pair_in, to_line, from_line, *refs):
+        p_send, p_recv, l_send, l_recv = refs[:4]
+        enter, send_core, select, send_grp, add_grps, send_z, add_lines = adapter_stages(
+            term_ref, id_ref, out_ref, refs[4:]
+        )
+        g, s = lax.axis_index("grp"), lax.axis_index("seq")
+        core, z = lax.rem(s, 2), s // 2
+        far_z = [lax.rem(z + d, blocks) for d in range(1, blocks)]
+        across = pltpu.make_async_remote_copy(
+            src_ref=x_ref.at[:, 1 - core],
+            dst_ref=pair_in,
+            send_sem=p_send,
+            recv_sem=p_recv,
+            device_id=(g, z * 2 + 1 - core),
+            device_id_type=MESH,
+        )
+        along = [
+            pltpu.make_async_remote_copy(
+                src_ref=to_line.at[d],
+                dst_ref=from_line.at[d],
+                send_sem=l_send.at[d],
+                recv_sem=l_recv.at[d],
+                device_id=(g, far * 2 + core),
+                device_id_type=MESH,
+            )
+            for d, far in enumerate(far_z)
+        ]
+        enter()
+        send_core()
+        across.start()
+        select()
+        send_grp()
+        across.wait()
+        for d, far in enumerate(far_z):
+            both = x_ref[far, core].astype(jnp.float32) + pair_in[far].astype(jnp.float32)
+            to_line[d] = both.astype(jnp.bfloat16)
+            along[d].start()
+        add_grps()
+        send_z()
+        total = x_ref[z, core].astype(jnp.float32) + pair_in[z].astype(jnp.float32)
+        for d, copy in enumerate(along):
+            copy.wait()
+            total = total + from_line[d].astype(jnp.float32)
+        sum_ref[...] = total
+        add_lines()
+
+    whole = pl.BlockSpec(memory_space=pltpu.VMEM)
+    return pl.pallas_call(
+        kernel,
+        in_specs=[whole] * 3,
+        out_specs=[whole] * 2,
+        out_shape=[
+            jax.ShapeDtypeStruct((rows, cols), jnp.float32),
+            jax.ShapeDtypeStruct((term_rows, 128), jnp.float32),
+        ],
+        scratch_shapes=[
+            pltpu.VMEM((blocks, rows, cols), jnp.bfloat16),
+            pltpu.VMEM((blocks - 1, rows, cols), jnp.bfloat16),
+            pltpu.VMEM((blocks - 1, rows, cols), jnp.bfloat16),
+            dma,
+            dma,
+            dma((blocks - 1,)),
+            dma((blocks - 1,)),
+        ]
+        + adapter_scratch(term_rows),
+        compiler_params=pltpu.CompilerParams(
+            collective_id=collective_id, has_side_effects=True, vmem_limit_bytes=VMEM_LIMIT
+        ),
+    )(rows_term, term, ident)
+
+
+def local_general(
     tokens,
     cotangent,
     query_key_value_weight,
@@ -319,6 +943,196 @@
     return (outputs, input_grad, down_grad, up_grad)
 
 
+def fast(
+    tokens,
+    cotangent,
+    query_key_value_weight,
+    attention_out_weight,
+    feedforward_in_weight,
+    feedforward_out_weight,
+    layer_norm_gains,
+    biases,
+    adapter_down_matrices,
+    adapter_up_matrices,
+    adapter_of_continuation,
+):
+    groups = (lax.axis_size("grp"), lax.axis_size("seq"))
+    prompt_rows = tokens.shape[0] - CONT_LEN
+    prompt_total = prompt_rows * groups[1]
+    down_rows = 3 * MODEL_WIDTH + HIDDEN_UNITS
+    up_cols = 5 * MODEL_WIDTH + HIDDEN_UNITS
+    adapter_index = adapter_of_continuation[0, 0]
+    shift_one = biases[:MODEL_WIDTH]
+    shift_two = biases[MODEL_WIDTH : 2 * MODEL_WIDTH]
+    bias_q = biases[2 * MODEL_WIDTH : 3 * MODEL_WIDTH]
+    bias_kv = jnp.concatenate(
+        [jnp.zeros((MODEL_WIDTH,), jnp.float32), biases[3 * MODEL_WIDTH : 4 * MODEL_WIDTH]]
+    )
+    bias_out = biases[4 * MODEL_WIDTH : 5 * MODEL_WIDTH]
+    bias_proj = biases[5 * MODEL_WIDTH : 6 * MODEL_WIDTH]
+    bias_fc = biases[6 * MODEL_WIDTH :]
+
+    prompt_tokens, w_qkv, downs, ups = gather_arrays(
+        groups,
+        [
+            tokens[:prompt_rows],
+            query_key_value_weight.reshape(-1, 3 * MODEL_WIDTH),
+            adapter_down_matrices.reshape(-1, 128),
+            adapter_up_matrices.reshape(-1, 128),
+        ],
+        [False, True, True, True],
+        [1, 2, 1, 1],
+        1,
+    )
+    down_all = lax.dynamic_index_in_dim(
+        downs.reshape(ADAPTER_COUNT, -1, 128), adapter_index, 0, keepdims=False
+    ).reshape(down_rows, ADAPTER_RANK)
+    up_all = lax.dynamic_index_in_dim(
+        ups.reshape(ADAPTER_COUNT, -1, 128), adapter_index, 0, keepdims=False
+    ).reshape(ADAPTER_RANK, up_cols)
+    down_qkv = down_all[:MODEL_WIDTH]
+    down_out = down_all[MODEL_WIDTH : 2 * MODEL_WIDTH]
+    down_fc = down_all[2 * MODEL_WIDTH : 3 * MODEL_WIDTH]
+    down_proj = down_all[3 * MODEL_WIDTH :]
+    up_qkv = up_all[:, : 3 * MODEL_WIDTH]
+    up_out = up_all[:, 3 * MODEL_WIDTH : 4 * MODEL_WIDTH]
+    up_fc = up_all[:, 4 * MODEL_WIDTH : 4 * MODEL_WIDTH + HIDDEN_UNITS]
+    up_proj = up_all[:, 4 * MODEL_WIDTH + HIDDEN_UNITS :]
+
+    inputs = tokens.astype(jnp.float32)
+    normed_own = layer_norm(inputs, layer_norm_gains[0], shift_one).astype(jnp.bfloat16)
+    normed_prompt = layer_norm(
+        prompt_tokens.astype(jnp.float32), layer_norm_gains[0], shift_one
+    ).astype(jnp.bfloat16)
+    normed_later = normed_own[prompt_rows:]
+    normed_keys = jnp.concatenate([normed_prompt, normed_later], 0)
+    inner_one = product(normed_later, down_qkv).astype(jnp.bfloat16)
+    queries = product(normed_own, w_qkv[:, :MODEL_WIDTH]) + bias_q
+    queries = queries.at[prompt_rows:].add(product(inner_one, up_qkv[:, :MODEL_WIDTH]))
+    queries = queries.astype(jnp.bfloat16)
+    keys_values = product(normed_keys, w_qkv[:, MODEL_WIDTH:]) + bias_kv
+    keys_values = keys_values.at[prompt_total:].add(product(inner_one, up_qkv[:, MODEL_WIDTH:]))
+    keys_values = keys_values.astype(jnp.bfloat16)
+
+    context, log_total, w_out, w_fc, w_proj = attend_and_gather(
+        groups,
+        queries,
+        keys_values,
+        [
+            attention_out_weight.reshape(-1, MODEL_WIDTH),
+            feedforward_in_weight.reshape(-1, HIDDEN_UNITS),
+            feedforward_out_weight.reshape(-1, MODEL_WIDTH),
+        ],
+        [1, 2, 2],
+        2,
+    )
+
+    inner_two = product(context[prompt_rows:], down_out).astype(jnp.bfloat16)
+    attention_output = product(context, w_out) + bias_out
+    attention_output = attention_output.at[prompt_rows:].add(product(inner_two, up_out))
+    hidden = inputs + attention_output
+    normed_two = layer_norm(hidden, layer_norm_gains[1], shift_two).astype(jnp.bfloat16)
+    inner_three = product(normed_two[prompt_rows:], down_fc).astype(jnp.bfloat16)
+    before_activation = product(normed_two, w_fc) + bias_fc
+    before_activation = before_activation.at[prompt_rows:].add(product(inner_three, up_fc))
+    activated = jax.nn.gelu(before_activation, approximate=True).astype(jnp.bfloat16)
+    inner_four = product(activated[prompt_rows:], down_proj).astype(jnp.bfloat16)
+    branch = product(activated, w_proj) + bias_proj
+    branch = branch.at[prompt_rows:].add(product(inner_four, up_proj))
+    outputs = (hidden + branch).astype(jnp.bfloat16)
+
+    later_cotangent = cotangent[prompt_rows:]
+    grad_inner_four = product_nt(later_cotangent, up_proj).astype(jnp.bfloat16)
+    grad_act = product_nt(cotangent, w_proj)
+    grad_act = grad_act.at[prompt_rows:].add(product_nt(grad_inner_four, down_proj))
+    gelu_pull = jax.vjp(lambda field: jax.nn.gelu(field, approximate=True), before_activation)[1]
+    grad_pre = gelu_pull(grad_act)[0].astype(jnp.bfloat16)
+    grad_inner_three = product_nt(grad_pre[prompt_rows:], up_fc).astype(jnp.bfloat16)
+    grad_normed_two = product_nt(grad_pre, w_fc)
+    grad_normed_two = grad_normed_two.at[prompt_rows:].add(product_nt(grad_inner_three, down_fc))
+    second_pull = jax.vjp(lambda field: layer_norm(field, layer_norm_gains[1], shift_two), hidden)[
+        1
+    ]
+    grad_hidden = cotangent.astype(jnp.float32) + second_pull(grad_normed_two)[0]
+    grad_attn = grad_hidden.astype(jnp.bfloat16)
+    grad_inner_two = product_nt(grad_attn[prompt_rows:], up_out).astype(jnp.bfloat16)
+    grad_context = product_nt(grad_attn, w_out)
+    grad_context = (
+        grad_context.at[prompt_rows:]
+        .add(product_nt(grad_inner_two, down_out))
+        .astype(jnp.bfloat16)
+    )
+
+    down_early = jnp.concatenate(
+        [
+            jnp.zeros((MODEL_WIDTH, ADAPTER_RANK), jnp.float32),
+            product_tn(context[prompt_rows:], grad_inner_two),
+            product_tn(normed_two[prompt_rows:], grad_inner_three),
+            product_tn(activated[prompt_rows:], grad_inner_four),
+        ],
+        0,
+    ).astype(jnp.bfloat16)
+    up_early = jnp.concatenate(
+        [
+            product_tn(inner_two, grad_attn[prompt_rows:]),
+            product_tn(inner_three, grad_pre[prompt_rows:]),
+            product_tn(inner_four, later_cotangent),
+        ],
+        1,
+    ).astype(jnp.bfloat16)
+    early_term = jnp.concatenate(
+        [down_early.reshape(4, -1, 128), up_early.reshape(4, -1, 128)], 1
+    )
+    ident = jnp.full((16, 128), adapter_index, jnp.int32).astype(jnp.bfloat16)
+
+    grad_q, grad_k, grad_v, early = attend_back_and_reduce(
+        queries, keys_values, grad_context, context, log_total, early_term, ident, 3
+    )
+
+    w_q, w_k, w_v = (
+        w_qkv[:, :MODEL_WIDTH],
+        w_qkv[:, MODEL_WIDTH : 2 * MODEL_WIDTH],
+        w_qkv[:, 2 * MODEL_WIDTH :],
+    )
+    rows_term = (
+        product_nt(grad_k[:prompt_total], w_k) + product_nt(grad_v[:prompt_total], w_v)
+    ).astype(jnp.bfloat16)
+    grad_later = jnp.concatenate(
+        [grad_q[prompt_rows:], grad_k[prompt_total:], grad_v[prompt_total:]], 1
+    )
+    grad_inner_one = product_nt(grad_later, up_qkv).astype(jnp.bfloat16)
+    down_late = product_tn(normed_later, grad_inner_one).astype(jnp.bfloat16)
+    up_late = product_tn(inner_one, grad_later).astype(jnp.bfloat16)
+    down_late = jnp.concatenate(
+        [
+            down_late.reshape(1, -1, 128),
+            jnp.zeros((3, MODEL_WIDTH * ADAPTER_RANK // 128, 128), jnp.bfloat16),
+        ],
+        0,
+    )
+    late_term = jnp.concatenate([down_late, up_late.reshape(4, -1, 128)], 1)
+    prompt_sum, late = last_exchange(
+        rows_term.reshape(groups[1] // 2, 2, prompt_rows, MODEL_WIDTH), late_term, ident, 4
+    )
+    later_normed_grad = product_nt(grad_later, w_qkv) + product_nt(grad_inner_one, down_qkv)
+    prompt_normed_grad = product_nt(grad_q[:prompt_rows], w_q) + prompt_sum
+    grad_normed_one = jnp.concatenate([prompt_normed_grad, later_normed_grad], 0)
+    first_pull = jax.vjp(lambda field: layer_norm(field, layer_norm_gains[0], shift_one), inputs)[1]
+    input_grad = grad_hidden + first_pull(grad_normed_one)[0]
+
+    split = down_rows * ADAPTER_RANK // 4 // 128
+    late_split = MODEL_WIDTH * ADAPTER_RANK // 128
+    down_grad = early[:split].at[:late_split].add(late[:late_split]).reshape(-1)
+    up_grad = jnp.concatenate(
+        [
+            late[late_split:].reshape(ADAPTER_RANK // 4, -1),
+            early[split:].reshape(ADAPTER_RANK // 4, -1),
+        ],
+        1,
+    ).reshape(-1)
+    return (outputs, input_grad, down_grad, up_grad)
+
+
 def solution(mesh):
     placed = (
         P(("grp", "seq"), None),
@@ -333,8 +1147,9 @@
         P(("grp", "seq")),
         P(("grp", "seq"), None),
     )
+    fits = mesh.shape["grp"] == 4 and mesh.shape["seq"] == 8
     return jax.shard_map(
-        local,
+        fast if fits else local_general,
         mesh=mesh,
         in_specs=placed,
         out_specs=(

time: 1110 us -> 462 us (0.42)
  waiting for transfers between devices: 466 us -> 0 us
  Pallas kernels: 0 us -> 271 us
  matrix products: 347 us -> 105 us
  local copies, waits for them, and re-layouts: 210 us -> 39.8 us
  other arithmetic: 59.6 us -> 38.5 us
  between operations: 15.9 us -> 2.56 us
    pallas_call x0 -> x4, Pallas kernels: none -> 271 us  [the longest x1 99.3 us: attend_and_gather(): pl.pallas_call(kernel, grid=(pairs,), in_specs=[pl.BlockSpec((rows, 128),...]
    all_gather x8 -> x0, waiting for transfers between devices: 243 us -> none  [the longest x1 65.9 us: local(): lax.all_gather(weight_shards[0], ('grp', 'seq'), axis=0, tiled=True)]
    unnamed x14 -> x0, waiting for transfers between devices: 223 us -> none
    dot_general x60 -> x15, matrix products: 176 us -> 51.4 us  [product_nt(): lax.dot_general(left_side, right_side, (((1,), (1,)), ((), ())), preferre...]
    dot_general x44 -> x14, matrix products: 110 us -> 47.3 us  [product(): return jnp.dot(left_side, right_side, preferred_element_type=jnp.float32)]
    reshape x6 -> x9, local copies, waits for them, and re-layouts: 60.8 us -> 5.38 us  [the longest x1 1.7 us: fast(): query_key_value_weight.reshape(-1, 3 * MODEL_WIDTH)]
    dot_general x40 -> x8, matrix products: 60.9 us -> 6.52 us  [product_tn(): lax.dot_general(left_side, right_side, (((0,), (0,)), ((), ())), preferre...]
    while x32 -> x0, local copies, waits for them, and re-layouts: 31 us -> none
  transfers between devices with their start and end apart: 11 -> 0, of which waited for: 9 -> 0; matrix products, arithmetic and copies ran while one was open for 25% -> 0% of each run, Pallas kernels for 0% -> 0%
where the time goes in v1:
time: 462 us; the launch traced here: 457 us
  Pallas kernels  271 us (59%)
  matrix products  105 us (23%)
  local copies, waits for them, and re-layouts  39.8 us (9%)
  other arithmetic  38.5 us (8%)
    pallas_call x1, Pallas kernels, attend_and_gather(): pl.pallas_call(kernel, grid=(pairs,), in_specs=[pl.BlockSpec((rows, 128),...  99.3 us
    pallas_call x1, Pallas kernels, gather_arrays(): pl.pallas_call(kernel, out_shape=shapes, in_specs=[pl.BlockSpec(memory_sp...  77.2 us
    pallas_call x1, Pallas kernels, attend_back_and_reduce(): pl.pallas_call(kernel, grid=(pairs,), in_specs=[row_spec, key_spec, pl.Bl...  57.4 us
    dot_general x15, matrix products, product_nt(): lax.dot_general(left_side, right_side, (((1,), (1,)), ((), ())), preferre...  51.4 us
    dot_general x14, matrix products, product(): return jnp.dot(left_side, right_side, preferred_element_type=jnp.float32)  47.3 us
    pallas_call x1, Pallas kernels, last_exchange(): pl.pallas_call(kernel, in_specs=[whole] * 3, out_specs=[whole] * 2, out_s...  37.3 us
    unnamed x96, local copies, waits for them, and re-layouts  14.7 us

profile of v1, /device:TPU:0, one launch (start us, length us, event | category | flops | bytes accessed | tf_op | source)
XLA Modules:
  0.0 457.3 jit_solution(16673651459653146423)
XLA Ops:
  2.3 1.7 reshape.346.refs_1_
  4.0 77.2 %shard_map.138 = (bf16[1024,1024]{1,0:T(8,128)(2,1)}, bf16[1024,3072]{1,0:T(8,128)(2,1)}, bf16[7168,128]{1,0:T(8,128)(2,1)}, bf16[9216,128]{1,0:T(8,128)(2,1)}) custom-call(bf16[128,1024]{1,0:T(8,128)(2,1)} %slice.320.refs_0_, bf16[32,3072]{1,0:T(8,128)(2,1)} %reshape.346.refs_1_, bf16[224,128]{1,0:T(8,128)(2,1)} %bitcast.79, bf16[288,128]{1,0:T(8,128)(2,1)} %bitcast.75), custom_call_target="tpu_custom_call" | custom-call | tf_op jit(solution)/shard_map/pallas_call | solution.py:250
  81.3 2.1 convert_reduce_fusion
  88.5 10.7 %convolution_add_fusion = f32[1536,2048]{1,0:T(8,128)} fusion(f32[2048]{0:T(1024)S(1)} %concatenate.51, bf16[1024,3072]{1,0:T(8,128)(2,1)S(1)} %copy-done.22, bf16[512,1024]{1,0:T(8,128)(2,1)S(1)} %slice.373, bf16[1024,1024]{1,0:T(8,128)(2,1)S(1)} %fusion.15), kind=kOutput, calls=%fused_computation.10 | convolution fusion | flops 6451888128 | bytes 19931136 | tf_op jit(solution)/shard_map/dot_general | solution.py:24
  101.2 1.7 constant_dynamic-slice_fusion.3
  104.0 4.9 %fusion.16 = f32[1536,2048]{1,0:T(8,128)} fusion(f32[1536,2048]{1,0:T(8,128)} %convolution_add_fusion, bf16[512,16]{0,1:T(8,128)(2,1)S(1)} %convolution_convert_fusion.13, bf16[16,9216]{1,0:T(8,128)(2,1)S(1)} %reshape.351), kind=kOutput, calls=%fused_computation.28 | convolution fusion | flops 34603008 | bytes 8470528 | tf_op jit(solution)/shard_map/dot_general | solution.py:24
  108.9 8.2 %convert_element_type.92.k_ref.v_ref = bf16[1536,2048]{1,0:T(8,128)(2,1)} convert(f32[1536,2048]{1,0:T(8,128)} %fusion.16) | non-fusion elementwise | flops 3145728 | bytes 18874368 | tf_op jit(solution)/shard_map/convert_element_type | solution.py:1015
  117.1 3.1 fusion.56
  124.3 99.3 %shard_map.139 = (bf16[640,1024]{1,0:T(8,128)(2,1)}, f32[640,1024]{1,0:T(8,128)}, bf16[1024,1024]{1,0:T(8,128)(2,1)}, bf16[1024,4096]{1,0:T(8,128)(2,1)}, bf16[4096,1024]{1,0:T(8,128)(2,1)}) custom-call(bf16[640,1024]{1,0:T(8,128)(2,1)} %convert_element_type.89.q_ref, bf16[1536,2048]{1,0:T(8,128)(2,1)} %convert_element_type.92.k_ref.v_ref, ...), custom_call_target="tpu_custom_call" | custom-call | tf_op jit(solution)/shard_map/pallas_call | solution.py:419
  223.6 8.5 %fusion.99 = f32[4096,640]{0,1:T(8,128)S(1)} fusion(bf16[4096,1024]{1,0:T(8,128)(2,1)} %get-tuple-element.134, bf16[640,1024]{1,0:T(8,128)(2,1)S(1)} %copy-done.7), kind=kOutput, calls=%fused_computation.154 | convolution fusion | flops 5368709120 | bytes 20185088 | tf_op jit(solution)/shard_map/dot_general | solution.py:34
  232.2 4.1 copy.29
  236.2 2.9 copy-done.3
  242.1 8.4 %fusion.8 = f32[640,4096]{1,0:T(8,128)} fusion(f32[640,4096]{1,0:T(8,128)} %copy.29, f32[4096,640]{0,1:T(8,128)} %copy-done.3, bf16[16,512]{1,0:T(8,128)(2,1)S(1)} %convolution_convert_fusion.10, bf16[4096,16]{1,0:T(8,128)(2,1)} %slice.350), kind=kOutput, calls=%fused_computation.13 | convolution fusion | flops 69206016 | bytes 17842176 | tf_op jit(solution)/shard_map/dot_general | solution.py:34
  252.3 3.5 convolution_add_fusion.4
  260.5 8.5 %convolution_add_fusion.1 = f32[640,4096]{1,0:T(8,128)S(1)} fusion(bf16[640,1024]{1,0:T(8,128)(2,1)} %add_convert_fusion.2, bf16[1024,4096]{1,0:T(8,128)(2,1)} %get-tuple-element.133, f32[4096]{0:T(1024)S(1)} %slice-done.5), kind=kOutput, calls=%fused_computation.16 | convolution fusion | flops 5371330560 | bytes 20201472 | tf_op jit(solution)/shard_map/dot_general | solution.py:24
  270.7 8.7 %fusion.6 = (bf16[640,4096]{1,0:T(8,128)(2,1)}, bf16[640,4096]{1,0:T(8,128)(2,1)S(1)}) fusion(f32[640,4096]{1,0:T(8,128)S(1)} %fusion.9, f32[640,4096]{1,0:T(8,128)S(1)} %bitcast.63), kind=kLoop, calls=%fused_computation.8 | loop fusion | flops 57671680 | bytes 31457280 | tf_op jit(solution)/shard_map/convert_element_type | solution.py:1049
  280.6 8.8 %convolution_add_fusion.3 = f32[640,1024]{1,0:T(8,128)S(1)} fusion(bf16[640,4096]{1,0:T(8,128)(2,1)S(1)} %get-tuple-element.147, bf16[4096,1024]{1,0:T(8,128)(2,1)} %get-tuple-element.134, f32[1024]{0:T(1024)S(1)} %copy-done.39), kind=kOutput, calls=%fused_computation.85 | convolution fusion | flops 5369364480 | bytes 16257024 | tf_op jit(solution)/shard_map/dot_general | solution.py:24
  291.1 5.6 %fusion.100 = f32[640,1024]{1,0:T(8,128)S(1)} fusion(bf16[640,4096]{1,0:T(8,128)(2,1)S(1)} %bitcast.66, bf16[1024,4096]{1,0:T(8,128)(2,1)S(1)} %bitcast.84), kind=kOutput, calls=%fused_computation.155 | convolution fusion | flops 5368709120 | bytes 16252928 | tf_op jit(solution)/shard_map/dot_general | solution.py:34
  299.1 2.0 fusion.95
  306.8 2.7 convert_element_type.106
  311.0 2.8 convolution_convert_fusion.1
  314.8 1.7 convert_element_type.107
  316.5 1.7 pad_maximum_fusion.1.term_ref
  318.3 3.5 fusion.101
  324.2 57.4 %shard_map.140 = (bf16[640,1024]{1,0:T(8,128)(2,1)}, bf16[1536,1024]{1,0:T(8,128)(2,1)}, bf16[1536,1024]{1,0:T(8,128)(2,1)}, f32[416,128]{1,0:T(8,128)}) custom-call(bf16[640,1024]{1,0:T(8,128)(2,1)} %convert_element_type.89.q_ref, bf16[1536,2048]{1,0:T(8,128)(2,1)} %convert_element_type.92.k_ref.v_ref, bf16[1536,2048]{1,0:T(8,128)(2,1)} %convert_element_type.92.k_ref.v_ref, ...), custom_call_target="tpu_custom_call" | custom-call | tf_op jit(solution)/shard_map/pallas_call | solution.py:606
  387.9 2.9 convolution_convert_fusion.8
  392.1 4.7 %fusion.41 = f32[1024,1024]{1,0:T(8,128)S(1)} fusion(bf16[1024,3072]{1,0:T(8,128)(2,1)} %get-tuple-element.127, bf16[1536,1024]{1,0:T(8,128)(2,1)} %get-tuple-element.138), kind=kOutput, calls=%fused_computation.73 | convolution fusion | flops 2147483648 | bytes 8388608 | tf_op jit(solution)/shard_map/dot_general | solution.py:34
  396.9 5.4 %add_convert_fusion = bf16[1024,1024]{1,0:T(8,128)(2,1)} fusion(f32[1024,1024]{1,0:T(8,128)S(1)} %fusion.41, bf16[1024,3072]{1,0:T(8,128)(2,1)} %get-tuple-element.127, bf16[1536,1024]{1,0:T(8,128)(2,1)S(1)} %copy-done.24), kind=kOutput, calls=%fused_computation.29 | convolution fusion | flops 2149580800 | bytes 10485760 | tf_op jit(solution)/shard_map/dot_general | solution.py:34
  402.2 37.3 %shard_map.141 = (f32[128,1024]{1,0:T(8,128)}, f32[224,128]{1,0:T(8,128)}) custom-call(bf16[4,2,128,1024]{3,2,1,0:T(8,128)(2,1)} %bitcast.67, bf16[4,224,128]{2,1,0:T(8,128)(2,1)} %fusion.78.term_ref, bf16[16,128]{1,0:T(8,128)(2,1)} %broadcast_in_dim.15.id_ref), custom_call_target="tpu_custom_call" | custom-call | tf_op jit(solution)/shard_map/pallas_call | solution.py:686
  442.3 2.6 fusion.59
  445.0 6.3 %fusion.93 = f32[512,1024]{1,0:T(8,128)S(1)} fusion(bf16[1024,3072]{1,0:T(8,128)(2,1)} %get-tuple-element.127, bf16[512,1024]{1,0:T(8,128)(2,1)S(1)} %copy-done.21, bf16[512,1024]{1,0:T(8,128)(2,1)S(1)} %copy-done.19, bf16[512,1024]{1,0:T(8,128)(2,1)S(1)} %copy-done.17), kind=kOutput, calls=%fused_computation.148 | convolution fusion | flops 3230662656 | bytes 11534336 | tf_op jit(solution)/shard_map/dot_general | solution.py:34
  454.4 2.4 add_add_fusion.2
  (178 shorter events, 53.2 us)
Async XLA Ops:
  2.3 81.9 %copy-start.35 = (f32[10240]{0:T(1024)S(1)}, f32[10240]{0:T(1024)}, u32[]{:S(2)}) copy-start(f32[10240]{0:T(1024)} %param.36) | copy-start | bytes 122884
  2.3 82.5 %copy-start.38 = (f32[2,1024]{1,0:T(2,128)S(1)}, f32[2,1024]{1,0:T(2,128)}, u32[]{:S(2)}) copy-start(f32[2,1024]{1,0:T(2,128)} %param.35) | copy-start | bytes 24580
  81.3 2.2 copy-start.6
  85.7 2.8 copy-start.22
  88.1 29.0 %copy-start.8 = (bf16[640,1024]{1,0:T(8,128)(2,1)}, bf16[640,1024]{1,0:T(8,128)(2,1)S(1)}, u32[]{:S(2)}) copy-start(bf16[640,1024]{1,0:T(8,128)(2,1)S(1)} %fusion.34) | copy-start | bytes 3932164
  100.8 8.1 %copy-start.14 = (bf16[1024,16]{1,0:T(8,128)(2,1)}, bf16[1024,16]{1,0:T(8,128)(2,1)S(1)}, u32[]{:S(2)}) copy-start(bf16[1024,16]{1,0:T(8,128)(2,1)S(1)} %slice.326) | copy-start | bytes 98308
  120.7 2.1 copy-start.26
  120.8 2.9 copy-start.34
  124.3 99.3 %copy-start.7 = (bf16[640,1024]{1,0:T(8,128)(2,1)S(1)}, bf16[640,1024]{1,0:T(8,128)(2,1)}, u32[]{:S(2)}) copy-start(bf16[640,1024]{1,0:T(8,128)(2,1)} %param.30) | copy-start | bytes 3932164
  232.2 7.0 %copy-start.3 = (f32[4096,640]{0,1:T(8,128)}, f32[4096,640]{0,1:T(8,128)S(1)}, u32[]{:S(2)}) copy-start(f32[4096,640]{0,1:T(8,128)S(1)} %fusion.99) | copy-start | bytes 31457284
  256.7 2.0 copy-start.1
  257.1 3.3 slice-start.5
  260.5 10.2 %slice-start = ((s8[10485760]{0:T(1024)(128)(4,1)}), s8[4194304]{0:T(1024)(128)(4,1)S(1)}, s32[]{:S(2)}) async-start(s8[10485760]{0:T(1024)(128)(4,1)} %bitcast.62), calls=%async_computation | async-start | bytes 8388608
  260.5 10.2 %slice-start.1 = ((s8[10485760]{0:T(1024)(128)(4,1)}), s8[4194304]{0:T(1024)(128)(4,1)S(1)}, s32[]{:S(2)}) async-start(s8[10485760]{0:T(1024)(128)(4,1)} %bitcast.62), calls=%async_computation.1 | async-start | bytes 8388608
  270.7 8.7 %copy-start.10 = (bf16[4096,16]{1,0:T(8,128)(2,1)S(1)}, bf16[4096,16]{1,0:T(8,128)(2,1)}, u32[]{:S(2)}) copy-start(bf16[4096,16]{1,0:T(8,128)(2,1)} %slice.350) | copy-start | bytes 393220
  279.3 10.6 %slice-start.3 = ((s8[5242880]{0:T(1024)(128)(4,1)}), s8[4194304]{0:T(1024)(128)(4,1)S(1)}, s32[]{:S(2)}) async-start(s8[5242880]{0:T(1024)(128)(4,1)} %bitcast.65), calls=%async_computation.3 | async-start | bytes 8388608
  279.3 11.8 %slice-start.6 = ((s8[8388608]{0:T(1024)(128)(4,1)}), s8[4194304]{0:T(1024)(128)(4,1)S(1)}, s32[]{:S(2)}) async-start(s8[8388608]{0:T(1024)(128)(4,1)} %bitcast.83), calls=%async_computation.6 | async-start | bytes 8388608
  280.5 9.4 %slice-start.4 = ((s8[5242880]{0:T(1024)(128)(4,1)}), s8[1048576]{0:T(1024)(128)(4,1)S(1)}, s32[]{:S(2)}) async-start(s8[5242880]{0:T(1024)(128)(4,1)} %bitcast.65), calls=%async_computation.4 | async-start | bytes 2097152
  280.5 10.6 %slice-start.7 = ((s8[8388608]{0:T(1024)(128)(4,1)}), s8[4194304]{0:T(1024)(128)(4,1)S(1)}, s32[]{:S(2)}) async-start(s8[8388608]{0:T(1024)(128)(4,1)} %bitcast.83), calls=%async_computation.7 | async-start | bytes 8388608
  296.8 1.7 copy-start.2
  301.1 2.3 copy-start.12
  301.1 3.1 copy-start.11
  302.6 2.6 copy-start.13
  382.9 3.4 copy-start.16
  387.8 2.9 copy-start.9
  392.1 4.7 %copy-start.24 = (bf16[1536,1024]{1,0:T(8,128)(2,1)S(1)}, bf16[1536,1024]{1,0:T(8,128)(2,1)}, u32[]{:S(2)}) copy-start(bf16[1536,1024]{1,0:T(8,128)(2,1)} %get-tuple-element.137) | copy-start | bytes 9437188
  396.9 43.5 %copy-start.23 = (f32[416,128]{1,0:T(8,128)S(1)}, f32[416,128]{1,0:T(8,128)}, u32[]{:S(2)}) copy-start(f32[416,128]{1,0:T(8,128)} %get-tuple-element.140) | copy-start | bytes 638980
  440.4 4.5 copy-start.17
  440.4 4.5 copy-start.19
  440.5 4.5 copy-start.21
  442.3 9.0 %copy-start.31 = (f32[224,128]{1,0:T(8,128)}, f32[224,128]{1,0:T(8,128)S(1)}, u32[]{:S(2)}) copy-start(f32[224,128]{1,0:T(8,128)S(1)} %add_dynamic-update-slice_fusion) | copy-start | bytes 344068
  445.0 6.3 %copy-start.15 = (bf16[1024,16]{1,0:T(8,128)(2,1)S(1)}, bf16[1024,16]{1,0:T(8,128)(2,1)}, u32[]{:S(2)}) copy-start(bf16[1024,16]{1,0:T(8,128)(2,1)} %copy-done.14) | copy-start | bytes 98308
  (16 other events, 17.6 us)
